TPU v7x, 128 devices: a whole 4x4x4 slice. The times are simulated.
128 devices in a mesh: tm: 32 (over z, x_lo, y), head: 4 (over x_hi, core).
Axes of the slice: x: 4 (x_hi: 2, x_lo: 2; x = x_hi * 2 + x_lo), y: 4, z: 4, core: 2. Of those that a mesh axis runs over, the one named last changes fastest.
Arguments:
- queries: bfloat16 [32768, 1024], P('tm', 'head'), may hold values from -8 to 8
- keys: bfloat16 [32768, 1024], P('tm', 'head'), may hold values from -8 to 8
- values: bfloat16 [32768, 1024], P('tm', 'head'), may hold values from -6 to 6
- out_weight: bfloat16 [1024, 1024], P('head'), may hold values from -0.1875 to 0.1875
- grad_output: bfloat16 [32768, 1024], P('tm'), may hold values from -6 to 6
- tile_lists: int32 [256, 5], P('tm'), may hold values from -1 to 255, as said below
Outputs:
- output: bfloat16 [32768, 1024], P('tm', 'head')
- grad_queries: bfloat16 [32768, 1024], P('tm', 'head')
- grad_keys: bfloat16 [32768, 1024], P('tm', 'head')
- grad_values: bfloat16 [32768, 1024], P('tm', 'head')
- grad_weight: float32 [1024, 1024], P('head', 'tm')
Inputs may be any that keep to these rules, and one draw needn't show every extreme that they name: `tile_lists`: the row of query tile b lists distinct key tiles t of b's recording session with b - 4 <= t <= b in falling order, the first entry b itself, then -1 in unused slots; the first tile of every stretch but the first lists the tile before it; in every draw some row uses all 5 slots.
All inputs are finite; a program needn't handle non-finite values.
Results may differ from a plain program's by a relative error of at most 0.0095.
Values may be sent and summed in bfloat16 or wider, within the bound.
No kernel may reach another device: no remote copies, remote signals or barrier semaphores. Data moves between devices by JAX's collectives and lax.ppermute only.
A program may use at most 128 MiB of HBM per device.

v0:
```python
import jax
import jax.numpy as jnp
from jax import lax
from jax.sharding import PartitionSpec as P

HD = 64
QB = 128


def from_behind(x, axis, by):
    devices = lax.axis_size(axis)
    pairs = [(i, i + by) for i in range(devices) if 0 <= i + by < devices]
    return lax.ppermute(x, axis, pairs)


def tile_allow(tile_rows, first_tile, span_tiles):
    tile_span = jnp.arange(2 * span_tiles, dtype=jnp.int32)
    wanted = first_tile[:, None] + tile_span[None, :]
    matched = (tile_rows[:, :, :, None] == wanted[:, None, None, :]) & (
        tile_rows[:, :, :, None] >= 0
    )
    return jnp.any(matched, axis=2)


def group_mask(allow_tiles, first_row, group_rows, span_rows):
    key_width = span_rows + group_rows
    tile_block = allow_tiles[
        :,
        first_row // QB : (first_row + group_rows) // QB,
        first_row // QB : (first_row + key_width) // QB,
    ]
    tile_block = jnp.repeat(jnp.repeat(tile_block, QB, axis=1), QB, axis=2)
    causal = jnp.arange(key_width)[None, :] <= jnp.arange(group_rows)[:, None] + span_rows
    return tile_block & causal[None]


def window_logits(q_group, k_group, allowed, score_scale):
    logits = (
        jnp.einsum("bqhd,bkhd->bhqk", q_group, k_group, preferred_element_type=jnp.float32)
        * score_scale
    )
    return jnp.where(allowed[:, None], logits, -1e30)


def on_device(queries, keys, values, out_weight, grad_output, tile_lists):
    feature_width = queries.shape[1]
    local_heads = feature_width // HD
    span_rows = queries.shape[0] // 2
    span_tiles = span_rows // QB
    group_rows = 256
    group_count = span_rows // group_rows
    score_scale = HD ** (-0.5)
    tm_count = lax.axis_size("tm")
    tm_index = lax.axis_index("tm")
    is_last = tm_index == tm_count - 1
    token_total = tm_count * queries.shape[0]
    q_half = queries.reshape(2, span_rows, local_heads, HD)
    k_half = keys.reshape(2, span_rows, local_heads, HD)
    v_half = values.reshape(2, span_rows, local_heads, HD)
    k_before_low, v_before_low = from_behind((k_half[0], v_half[0]), "tm", 1)
    k_recv_high, v_recv_high = from_behind((k_half[1], v_half[1]), "tm", -1)
    k_before_high = jnp.where(is_last, k_half[0], k_recv_high)
    v_before_high = jnp.where(is_last, v_half[0], v_recv_high)
    k_window = jnp.stack(
        [
            jnp.concatenate([k_before_low, k_half[0]], axis=0),
            jnp.concatenate([k_before_high, k_half[1]], axis=0),
        ]
    )
    v_window = jnp.stack(
        [
            jnp.concatenate([v_before_low, v_half[0]], axis=0),
            jnp.concatenate([v_before_high, v_half[1]], axis=0),
        ]
    )
    piece_ids = jnp.stack([tm_index, 2 * tm_count - 1 - tm_index])
    first_tile = (piece_ids - 1) * span_tiles
    allow_tiles = tile_allow(tile_lists.reshape(2, span_tiles, -1), first_tile, span_tiles)
    out_parts = []
    log_parts = []
    masks = []
    for block_index in range(group_count):
        first_row = block_index * group_rows
        allowed = group_mask(allow_tiles, first_row, group_rows, span_rows)
        masks.append(allowed)
        q_group = q_half[:, first_row : first_row + group_rows]
        k_group = k_window[:, first_row : first_row + span_rows + group_rows]
        v_group = v_window[:, first_row : first_row + span_rows + group_rows]
        logits = window_logits(q_group, k_group, allowed, score_scale)
        row_max = jnp.max(logits, axis=-1, keepdims=True)
        probability = jnp.exp(logits - row_max)
        row_total = jnp.sum(probability, axis=-1)
        mixture = jnp.einsum(
            "bhqk,bkhd->bqhd",
            probability.astype(jnp.bfloat16),
            v_group,
            preferred_element_type=jnp.float32,
        )
        total_rows = jnp.transpose(row_total, (0, 2, 1))[..., None]
        out_parts.append((mixture / total_rows).astype(jnp.bfloat16))
        log_parts.append(row_max[..., 0] + jnp.log(row_total))
    attended = jnp.concatenate(out_parts, axis=1)
    attended_flat = attended.reshape(2 * span_rows, feature_width)
    partial_value = jnp.dot(attended_flat, out_weight, preferred_element_type=jnp.float32)
    summed = lax.psum_scatter(partial_value, "head", scatter_dimension=1, tiled=True)
    output = summed.astype(jnp.bfloat16)
    grad_attn = lax.dot_general(
        grad_output, out_weight, (((1,), (1,)), ((), ())), preferred_element_type=jnp.float32
    ).astype(jnp.bfloat16)
    weight_term = lax.dot_general(
        attended_flat, grad_output, (((0,), (0,)), ((), ())), preferred_element_type=jnp.float32
    )
    grad_weight = lax.psum_scatter(
        weight_term, "tm", scatter_dimension=1, tiled=True
    ) * token_total ** (-0.5)
    g_half = grad_attn.reshape(2, span_rows, local_heads, HD)
    row_delta = jnp.sum(g_half.astype(jnp.float32) * attended.astype(jnp.float32), axis=-1)
    dk_window = jnp.zeros((2, 2 * span_rows, local_heads, HD), jnp.float32)
    dv_window = jnp.zeros((2, 2 * span_rows, local_heads, HD), jnp.float32)
    dq_parts = []
    for block_index in range(group_count):
        first_row = block_index * group_rows
        last_key = first_row + span_rows + group_rows
        q_group = q_half[:, first_row : first_row + group_rows]
        k_group = k_window[:, first_row:last_key]
        v_group = v_window[:, first_row:last_key]
        g_group = g_half[:, first_row : first_row + group_rows]
        logits = window_logits(q_group, k_group, masks[block_index], score_scale)
        back_prob = jnp.exp(logits - log_parts[block_index][..., None])
        back_round = back_prob.astype(jnp.bfloat16)
        dv_part = jnp.einsum(
            "bhqk,bqhd->bkhd", back_round, g_group, preferred_element_type=jnp.float32
        )
        dprob = jnp.einsum("bqhd,bkhd->bhqk", g_group, v_group, preferred_element_type=jnp.float32)
        delta_group = jnp.transpose(row_delta[:, first_row : first_row + group_rows], (0, 2, 1))[
            ..., None
        ]
        dscore_round = (back_prob * (dprob - delta_group)).astype(jnp.bfloat16)
        dq_parts.append(
            jnp.einsum("bhqk,bkhd->bqhd", dscore_round, k_group, preferred_element_type=jnp.float32)
            * score_scale
        )
        dk_part = (
            jnp.einsum("bhqk,bqhd->bkhd", dscore_round, q_group, preferred_element_type=jnp.float32)
            * score_scale
        )
        dk_window = dk_window.at[:, first_row:last_key].add(dk_part)
        dv_window = dv_window.at[:, first_row:last_key].add(dv_part)
    dk_down, dv_down = from_behind((dk_window[0, :span_rows], dv_window[0, :span_rows]), "tm", -1)
    dk_up, dv_up = from_behind((dk_window[1, :span_rows], dv_window[1, :span_rows]), "tm", 1)
    dk_low = dk_window[0, span_rows:] + jnp.where(is_last, dk_window[1, :span_rows], dk_down)
    dv_low = dv_window[0, span_rows:] + jnp.where(is_last, dv_window[1, :span_rows], dv_down)
    dk_high = dk_window[1, span_rows:] + dk_up
    dv_high = dv_window[1, span_rows:] + dv_up
    grad_keys = (
        jnp.concatenate([dk_low, dk_high], axis=0)
        .reshape(2 * span_rows, feature_width)
        .astype(jnp.bfloat16)
    )
    grad_values = (
        jnp.concatenate([dv_low, dv_high], axis=0)
        .reshape(2 * span_rows, feature_width)
        .astype(jnp.bfloat16)
    )
    grad_queries = (
        jnp.concatenate(dq_parts, axis=1).reshape(2 * span_rows, feature_width).astype(jnp.bfloat16)
    )
    return (output, grad_queries, grad_keys, grad_values, grad_weight)


def solution(mesh):
    return jax.shard_map(
        on_device,
        mesh=mesh,
        in_specs=(
            P("tm", "head"),
            P("tm", "head"),
            P("tm", "head"),
            P("head", None),
            P("tm", None),
            P("tm", None),
        ),
        out_specs=(
            P("tm", "head"),
            P("tm", "head"),
            P("tm", "head"),
            P("tm", "head"),
            P("head", "tm"),
        ),
        check_vma=False,
    )
```

profile of v0, /device:TPU:32, one launch (start us, length us, event | category | flops | bytes accessed | tf_op | source)
XLA Modules:
  0.0 279.7 jit_solution(8281436161239510732)
XLA Ops:
  9.3 5.4 %collective-permute-start.3 = (bf16[512,4,64]{0,2,1:T(8,128)(2,1)}, bf16[512,4,64]{0,2,1:T(8,128)(2,1)}, u32[]{:S(2)}, u32[]{:S(2)}) collective-permute-start(bf16[512,4,64]{0,2,1:T(8,128)(2,1)} %bitcast.11), channel_id=1, source_target_pairs={{4,0},{8,4},{12,8},{16,12},{20,16},{24,20},{28,24},{32,28},{36,32}... | collective-permute-start | bytes 786440 | tf_op jit(solution)/shard_map/ppermute | solution.py:13
  15.5 1.9 collective-permute-start.2
  19.3 6.9 %collective-permute-start.1 = (bf16[512,4,64]{0,2,1:T(8,128)(2,1)}, bf16[512,4,64]{0,2,1:T(8,128)(2,1)}, u32[]{:S(2)}, u32[]{:S(2)}) collective-permute-start(bf16[512,4,64]{0,2,1:T(8,128)(2,1)} %bitcast.2), channel_id=1, source_target_pairs={{4,0},{8,4},{12,8},{16,12},{20,16},{24,20},{28,24},{32,28},{36,32}... | collective-permute-start | bytes 786440 | tf_op jit(solution)/shard_map/ppermute | solution.py:13
  27.1 1.9 collective-permute-start
  29.6 2.2 reshape.286
  41.1 1.4 fusion.2
  43.8 1.4 fusion
  48.7 1.6 fusion.44
  50.4 1.6 fusion.50
  52.8 1.9 fusion.91
  55.0 3.7 %fusion.90 = f32[1024,1024]{1,0:T(8,128)} fusion(bf16[1024,256]{0,1:T(8,128)(2,1)S(1)} %bitcast.165, bf16[256,1024]{1,0:T(8,128)(2,1)} %param.17), kind=kOutput, calls=%fused_computation.122 | convolution fusion | flops 536870912 | bytes 5242880 | tf_op jit(solution)/shard_map/dot_general | solution.py:104
  59.7 1.5 convolution_convert_fusion
  61.3 2.0 reshape.287
  64.6 1.5 multiply_reduce_fusion
  66.9 5.4 %multiply_convert_fusion.1 = bf16[2,4,256,768]{2,3,1,0:T(8,128)(2,1)S(1)} fusion(f32[2,4,768,256]{3,2,1,0:T(8,128)} %copy-done.4, f32[2,4,256]{2,1,0:T(4,128)S(1)} %get-tuple-element.84, f32[2,4,256]{2,1,0:T(4,128)S(1)} %bitcast.181, pred[2,256,768]{1,2,0:T(8,128)(4,1)} %copy-done.10, bf16[2,512,4,64]{1,3,2,0:T(8,128)(2,1)} %copy.66, ...), kind=kOutput, calls=%fused_computation.4 | convolution fusion | flops 211156992 | bytes 11157504 | tf_op jit(solution)/shard_map/bqhd,bkhd->bhqk/dot_general | solution.py:134
  73.8 2.5 multiply_convert_fusion
  76.3 2.2 constant_dynamic-update-slice_fusion.1
  79.8 6.9 %collective-permute-start.4 = (f32[512,4,64]{0,2,1:T(8,128)}, f32[512,4,64]{0,2,1:T(8,128)}, u32[]{:S(2)}, u32[]{:S(2)}) collective-permute-start(f32[512,4,64]{0,2,1:T(8,128)} %get-tuple-element.70), channel_id=1, source_target_pairs={{4,0},{8,4},{12,8},{16,12},{20,16},{24,20},{28,24},{32,28},{36,32}... | collective-permute-start | bytes 1572872 | tf_op jit(solution)/shard_map/ppermute | solution.py:13
  86.7 2.1 collective-permute-start.5
  88.8 1.9 fusion.26
  91.7 3.0 %constant_dynamic-update-slice_fusion = (f32[2,1024,4,64]{1,3,2,0:T(8,128)S(1)}, f32[2,768,4,64]{1,3,2,0:T(8,128)}) fusion(f32[2,1024,4,64]{1,3,2,0:T(8,128)S(1)} %scatter-add.16, f32[2,4,768,256]{3,2,1,0:T(8,128)S(1)} %bitcast.163, f32[2,4,256]{2,1,0:T(4,128)S(1)} %bitcast.178, pred[2,256,768]{1,2,0:T(8,128)(4,1)S(1)} %get-tuple-element.83, ...), kind=kOutput, calls=%fused_computation.101 | convolution fusion | flops 208011264 | bytes 11673600 | tf_op jit(solution)/shard_map/bhqk,bqhd->bkhd/dot_general | solution.py:131
  95.9 6.9 %collective-permute-start.6 = (f32[512,4,64]{0,2,1:T(8,128)}, f32[512,4,64]{0,2,1:T(8,128)}, u32[]{:S(2)}, u32[]{:S(2)}) collective-permute-start(f32[512,4,64]{0,2,1:T(8,128)} %get-tuple-element.68), channel_id=1, source_target_pairs={{4,0},{8,4},{12,8},{16,12},{20,16},{24,20},{28,24},{32,28},{36,32}... | collective-permute-start | bytes 1572872 | tf_op jit(solution)/shard_map/ppermute | solution.py:13
  102.9 2.2 collective-permute-start.7
  106.5 1.6 copy.91
  108.2 1.5 reshape.285
  109.6 1.9 fusion.62
  113.6 7.2 %collective-permute-done.7 = f32[512,4,64]{0,2,1:T(8,128)} collective-permute-done((f32[512,4,64]{0,2,1:T(8,128)}, f32[512,4,64]{0,2,1:T(8,128)}, u32[]{:S(2)}, u32[]{:S(2)}) %collective-permute-start.7) | collective-permute-done | bytes 524320 | tf_op jit(solution)/shard_map/ppermute | solution.py:13
  120.8 1.9 fusion.58
  123.7 82.3 %reduce-scatter.5.cloned.1.call-done = f32[256,32]{0,1:T(8,128)} async-done(((f32[256,1024]{0,1:T(8,128)}), f32[256,32]{0,1:T(8,128)}) %reduce-scatter.5.cloned.1.call-update) | async-done | bytes 32784 | tf_op jit(solution)/shard_map/reduce_scatter | solution.py:113
  206.0 1.4 broadcast_multiply_fusion
  207.4 63.4 %reduce-scatter.3.cloned.1.call-done = f32[1024,256]{1,0:T(8,128)} async-done(((f32[1024,1024]{1,0:T(8,128)}), f32[1024,256]{1,0:T(8,128)}) %reduce-scatter.3.cloned.1.call-update) | async-done | bytes 1048592 | tf_op jit(solution)/shard_map/reduce_scatter | solution.py:105
  270.8 2.1 convert_element_type.52
  (120 shorter events, 33.6 us)
Async XLA Ops:
  7.2 45.6 %copy-start = (bf16[1024,1024]{1,0:T(8,128)(2,1)S(1)}, bf16[1024,1024]{1,0:T(8,128)(2,1)}, u32[]{:S(2)}) copy-start(bf16[1024,1024]{1,0:T(8,128)(2,1)} %param.18) | copy-start | bytes 6291460
  7.2 21.8 %copy-start.25 = (s32[8,5]{1,0:T(8,128)S(1)}, s32[8,5]{1,0:T(8,128)}, u32[]{:S(2)}) copy-start(s32[8,5]{1,0:T(8,128)} %param.19) | copy-start | bytes 484
  7.2 198.8 %reduce-scatter.5.cloned.1.call-start = ((), (), s32[]{:S(2)}) async-start(), calls=%async_computation.3 | async-start | bytes 1081344 | tf_op jit(solution)/shard_map/reduce_scatter | solution.py:113
  9.3 27.1 %collective-permute-start.3 = (bf16[512,4,64]{0,2,1:T(8,128)(2,1)}, bf16[512,4,64]{0,2,1:T(8,128)(2,1)}, u32[]{:S(2)}, u32[]{:S(2)}) collective-permute-start(bf16[512,4,64]{0,2,1:T(8,128)(2,1)} %bitcast.11), channel_id=1, source_target_pairs={{4,0},{8,4},{12,8},{16,12},{20,16},{24,20},{28,24},{32,28},{36,32}... | collective-permute-start | bytes 786440 | tf_op jit(solution)/shard_map/ppermute | solution.py:13
  15.5 23.0 %collective-permute-start.2 = (bf16[512,4,64]{0,2,1:T(8,128)(2,1)}, bf16[512,4,64]{0,2,1:T(8,128)(2,1)}, u32[]{:S(2)}, u32[]{:S(2)}) collective-permute-start(bf16[512,4,64]{0,2,1:T(8,128)(2,1)} %bitcast.9), channel_id=1, source_target_pairs={{0,4},{4,8},{8,12},{12,16},{16,20},{20,24},{24,28},{28,32},{32,36}... | collective-permute-start | bytes 786440 | tf_op jit(solution)/shard_map/ppermute | solution.py:13
  19.3 25.9 %collective-permute-start.1 = (bf16[512,4,64]{0,2,1:T(8,128)(2,1)}, bf16[512,4,64]{0,2,1:T(8,128)(2,1)}, u32[]{:S(2)}, u32[]{:S(2)}) collective-permute-start(bf16[512,4,64]{0,2,1:T(8,128)(2,1)} %bitcast.2), channel_id=1, source_target_pairs={{4,0},{8,4},{12,8},{16,12},{20,16},{24,20},{28,24},{32,28},{36,32}... | collective-permute-start | bytes 786440 | tf_op jit(solution)/shard_map/ppermute | solution.py:13
  27.1 20.3 %collective-permute-start = (bf16[512,4,64]{0,2,1:T(8,128)(2,1)}, bf16[512,4,64]{0,2,1:T(8,128)(2,1)}, u32[]{:S(2)}, u32[]{:S(2)}) collective-permute-start(bf16[512,4,64]{0,2,1:T(8,128)(2,1)} %bitcast), channel_id=1, source_target_pairs={{0,4},{4,8},{8,12},{12,16},{16,20},{20,24},{24,28},{28,32},{32,36}... | collective-permute-start | bytes 786440 | tf_op jit(solution)/shard_map/ppermute | solution.py:13
  34.5 8.0 %copy-start.14 = (bf16[2,256,4,64]{1,3,2,0:T(8,128)(2,1)}, bf16[2,256,4,64]{1,3,2,0:T(8,128)(2,1)S(1)}, u32[]{:S(2)}) copy-start(bf16[2,256,4,64]{1,3,2,0:T(8,128)(2,1)S(1)} %copy.97) | copy-start | bytes 786436
  35.8 5.2 %copy-start.12 = (bf16[2,256,4,64]{1,3,2,0:T(8,128)(2,1)}, bf16[2,256,4,64]{1,3,2,0:T(8,128)(2,1)S(1)}, u32[]{:S(2)}) copy-start(bf16[2,256,4,64]{1,3,2,0:T(8,128)(2,1)S(1)} %copy.98) | copy-start | bytes 786436
  36.3 14.0 %copy-start.10 = (pred[2,256,768]{1,2,0:T(8,128)(4,1)}, pred[2,256,768]{1,2,0:T(8,128)(4,1)S(1)}, u32[]{:S(2)}) copy-start(pred[2,256,768]{1,2,0:T(8,128)(4,1)S(1)} %get-tuple-element.82) | copy-start | bytes 1179652
  38.5 4.0 %copy-start.6 = (bf16[1,1024,4,64]{1,3,2,0:T(8,128)(2,1)}, bf16[1,1024,4,64]{1,3,2,0:T(8,128)(2,1)S(1)}, u32[]{:S(2)}) copy-start(bf16[1,1024,4,64]{1,3,2,0:T(8,128)(2,1)S(1)} %maximum_bitcast_fusion.3) | copy-start | bytes 1572868
  39.8 2.7 copy-start.8
  41.1 7.6 %copy-start.1 = (f32[2,4,768,256]{3,2,1,0:T(8,128)}, f32[2,4,768,256]{3,2,1,0:T(8,128)S(1)}, u32[]{:S(2)}) copy-start(f32[2,4,768,256]{3,2,1,0:T(8,128)S(1)} %get-tuple-element.89) | copy-start | bytes 18874372
  43.8 6.6 %copy-start.4 = (f32[2,4,768,256]{3,2,1,0:T(8,128)}, f32[2,4,768,256]{3,2,1,0:T(8,128)S(1)}, u32[]{:S(2)}) copy-start(f32[2,4,768,256]{3,2,1,0:T(8,128)S(1)} %get-tuple-element.91) | copy-start | bytes 18874372
  43.8 6.6 %copy-start.23 = (f32[2,4,256]{2,1,0:T(4,128)}, f32[2,4,256]{2,1,0:T(4,128)S(1)}, u32[]{:S(2)}) copy-start(f32[2,4,256]{2,1,0:T(4,128)S(1)} %get-tuple-element.90) | copy-start | bytes 24580
  45.2 5.2 %copy-start.24 = (f32[2,4,256]{2,1,0:T(4,128)}, f32[2,4,256]{2,1,0:T(4,128)S(1)}, u32[]{:S(2)}) copy-start(f32[2,4,256]{2,1,0:T(4,128)S(1)} %fusion) | copy-start | bytes 24580
  47.4 3.0 %copy-start.19 = (bf16[1,1024,4,64]{1,3,2,0:T(8,128)(2,1)}, bf16[1,1024,4,64]{1,3,2,0:T(8,128)(2,1)S(1)}, u32[]{:S(2)}) copy-start(bf16[1,1024,4,64]{1,3,2,0:T(8,128)(2,1)S(1)} %maximum_bitcast_fusion.1) | copy-start | bytes 1572868
  54.7 216.1 %reduce-scatter.3.cloned.1.call-start = ((), (), s32[]{:S(2)}) async-start(), calls=%async_computation.2 | async-start | bytes 5242880 | tf_op jit(solution)/shard_map/reduce_scatter | solution.py:105
  64.6 9.1 %slice-start = ((s8[6291456]{0:T(1024)(128)(4,1)}), s8[4194304]{0:T(1024)(128)(4,1)S(1)}, s32[]{:S(2)}) async-start(s8[6291456]{0:T(1024)(128)(4,1)} %bitcast.162), calls=%async_computation.4 | async-start | bytes 8388608
  66.9 5.4 %copy-start.15 = (bf16[2,256,4,64]{1,3,2,0:T(8,128)(2,1)S(1)}, bf16[2,256,4,64]{1,3,2,0:T(8,128)(2,1)}, u32[]{:S(2)}) copy-start(bf16[2,256,4,64]{1,3,2,0:T(8,128)(2,1)} %copy-done.14) | copy-start | bytes 786436
  66.9 6.8 %slice-start.1 = ((s8[6291456]{0:T(1024)(128)(4,1)}), s8[2097152]{0:T(1024)(128)(4,1)S(1)}, s32[]{:S(2)}) async-start(s8[6291456]{0:T(1024)(128)(4,1)} %bitcast.162), calls=%async_computation.5 | async-start | bytes 4194304
  73.5 15.3 %slice-start.2 = ((s8[6291456]{0:T(1024)(128)(4,1)}), s8[4194304]{0:T(1024)(128)(4,1)S(1)}, s32[]{:S(2)}) async-start(s8[6291456]{0:T(1024)(128)(4,1)} %bitcast.166), calls=%async_computation.6 | async-start | bytes 8388608
  73.8 15.0 %slice-start.3 = ((s8[6291456]{0:T(1024)(128)(4,1)}), s8[2097152]{0:T(1024)(128)(4,1)S(1)}, s32[]{:S(2)}) async-start(s8[6291456]{0:T(1024)(128)(4,1)} %bitcast.166), calls=%async_computation.7 | async-start | bytes 4194304
  76.3 12.5 %copy-start.11 = (pred[2,256,768]{1,2,0:T(8,128)(4,1)S(1)}, pred[2,256,768]{1,2,0:T(8,128)(4,1)}, u32[]{:S(2)}) copy-start(pred[2,256,768]{1,2,0:T(8,128)(4,1)} %copy-done.10) | copy-start | bytes 1179652
  78.6 12.2 %copy-start.2 = (f32[2,1024,4,64]{1,3,2,0:T(8,128)}, f32[2,1024,4,64]{1,3,2,0:T(8,128)S(1)}, u32[]{:S(2)}) copy-start(f32[2,1024,4,64]{1,3,2,0:T(8,128)S(1)} %get-tuple-element.92) | copy-start | bytes 6291460
  79.8 29.9 %collective-permute-start.4 = (f32[512,4,64]{0,2,1:T(8,128)}, f32[512,4,64]{0,2,1:T(8,128)}, u32[]{:S(2)}, u32[]{:S(2)}) collective-permute-start(f32[512,4,64]{0,2,1:T(8,128)} %get-tuple-element.70), channel_id=1, source_target_pairs={{4,0},{8,4},{12,8},{16,12},{20,16},{24,20},{28,24},{32,28},{36,32}... | collective-permute-start | bytes 1572872 | tf_op jit(solution)/shard_map/ppermute | solution.py:13
  86.7 4.3 %copy-start.7 = (bf16[1,1024,4,64]{1,3,2,0:T(8,128)(2,1)S(1)}, bf16[1,1024,4,64]{1,3,2,0:T(8,128)(2,1)}, u32[]{:S(2)}) copy-start(bf16[1,1024,4,64]{1,3,2,0:T(8,128)(2,1)} %copy-done.6) | copy-start | bytes 1572868
  86.7 4.3 %copy-start.9 = (bf16[1,1024,4,64]{1,3,2,0:T(8,128)(2,1)S(1)}, bf16[1,1024,4,64]{1,3,2,0:T(8,128)(2,1)}, u32[]{:S(2)}) copy-start(bf16[1,1024,4,64]{1,3,2,0:T(8,128)(2,1)} %copy-done.8) | copy-start | bytes 1572868
  86.7 22.9 %collective-permute-start.5 = (f32[512,4,64]{0,2,1:T(8,128)}, f32[512,4,64]{0,2,1:T(8,128)}, u32[]{:S(2)}, u32[]{:S(2)}) collective-permute-start(f32[512,4,64]{0,2,1:T(8,128)} %get-tuple-element.71), channel_id=1, source_target_pairs={{0,4},{4,8},{8,12},{12,16},{16,20},{20,24},{24,28},{28,32},{32,36}... | collective-permute-start | bytes 1572872 | tf_op jit(solution)/shard_map/ppermute | solution.py:13
  94.7 11.0 %copy-start.3 = (f32[2,1024,4,64]{1,3,2,0:T(8,128)}, f32[2,1024,4,64]{1,3,2,0:T(8,128)S(1)}, u32[]{:S(2)}) copy-start(f32[2,1024,4,64]{1,3,2,0:T(8,128)S(1)} %get-tuple-element.94) | copy-start | bytes 6291460
  95.9 17.7 %collective-permute-start.6 = (f32[512,4,64]{0,2,1:T(8,128)}, f32[512,4,64]{0,2,1:T(8,128)}, u32[]{:S(2)}, u32[]{:S(2)}) collective-permute-start(f32[512,4,64]{0,2,1:T(8,128)} %get-tuple-element.68), channel_id=1, source_target_pairs={{4,0},{8,4},{12,8},{16,12},{20,16},{24,20},{28,24},{32,28},{36,32}... | collective-permute-start | bytes 1572872 | tf_op jit(solution)/shard_map/ppermute | solution.py:13
  102.9 17.9 %collective-permute-start.7 = (f32[512,4,64]{0,2,1:T(8,128)}, f32[512,4,64]{0,2,1:T(8,128)}, u32[]{:S(2)}, u32[]{:S(2)}) collective-permute-start(f32[512,4,64]{0,2,1:T(8,128)} %get-tuple-element.69), channel_id=1, source_target_pairs={{0,4},{4,8},{8,12},{12,16},{16,20},{20,24},{24,28},{28,32},{32,36}... | collective-permute-start | bytes 1572872 | tf_op jit(solution)/shard_map/ppermute | solution.py:13
  (8 other events, 11.8 us)
Sparse Core Ops, SparseCore 0:
  54.8 151.1 reduce-scatter.4
  208.6 62.1 reduce-scatter.2
where the time goes:
time: 282 us; the launch traced here: 280 us
  waiting for transfers between devices  154 us (55%)
  starting transfers between devices  34.5 us (12%)
  matrix products  30.4 us (11%)
  local copies, waits for them, and re-layouts  25.2 us (9%)
  other arithmetic  20.8 us (7%)
  between operations  14.8 us (5%)
    reduce_scatter x1, waiting for transfers between devices, on_device(): lax.psum_scatter(weight_term, 'tm', scatter_dimension=1, tiled=True)  82.3 us
    reduce_scatter x1, waiting for transfers between devices, on_device(): lax.psum_scatter(partial_value, 'head', scatter_dimension=1, tiled=True)  63.4 us
    ppermute x8, starting transfers between devices, from_behind(): return lax.ppermute(x, axis, pairs)  34.2 us
    unnamed x67, local copies, waits for them, and re-layouts  8.89 us
    ppermute x8, waiting for transfers between devices, from_behind(): return lax.ppermute(x, axis, pairs)  8.2 us
    dot_general x2, matrix products, on_device(): jnp.einsum('bqhd,bkhd->bhqk', g_group, v_group, preferred_element_type=jn...  7.89 us
  transfers between devices with their start and end apart: 10, of which 4 were waited for; matrix products, arithmetic and copies ran while one was open for 23% of the time, Pallas kernels for 0%

commit v1 on v0

v1 whole, which is shorter than its diff:
```python
import functools

import jax
import jax.numpy as jnp
from jax import lax
from jax.experimental import pallas as pl
from jax.experimental.pallas import tpu as pltpu
from jax.sharding import PartitionSpec as P

HD = 64
QB = 128
REACH = 5
NEG = -1e30


def dot(a, b, ca, cb):
    return lax.dot_general(a, b, (((ca,), (cb,)), ((), ())), preferred_element_type=jnp.float32)


def attention_kernel(
    allow_ref, flag_ref, q_ref, k_ref, v_ref, kvp_ref, kl_ref, vl_ref, g_ref,
    att_ref, dq_ref, dkvp_ref, dko_ref, dvo_ref,
    kwin, vwin, kt, vt, dk, dv, *, high,
):
    span, width = q_ref.shape
    heads = width // HD
    tiles = span // QB
    reach = REACH * QB
    if high:
        last = flag_ref[0] > 0

        @pl.when(last)
        def _():
            kwin[:span] = kl_ref[...]
            vwin[:span] = vl_ref[...]

        @pl.when(jnp.logical_not(last))
        def _():
            kwin[:span] = kvp_ref[:span]
            vwin[:span] = kvp_ref[span:]
    else:
        kwin[:span] = kvp_ref[:span]
        vwin[:span] = kvp_ref[span:]
    kwin[span:] = k_ref[...]
    vwin[span:] = v_ref[...]
    kt[...] = kwin[...].T
    vt[...] = vwin[...].T
    dk[...] = jnp.zeros_like(dk)
    dv[...] = jnp.zeros_like(dv)
    head_of = lax.broadcasted_iota(jnp.int32, (1, width), 1) // HD
    head_masks = [(head_of == h).astype(jnp.float32) for h in range(heads)]
    key_row = lax.broadcasted_iota(jnp.int32, (QB, heads * QB), 0)
    query_col = lax.broadcasted_iota(jnp.int32, (QB, heads * QB), 1) % QB
    causal = jnp.where(key_row <= query_col, 0.0, NEG)

    def stacked(x):
        return jnp.concatenate([(x * m).astype(jnp.bfloat16) for m in head_masks], axis=0)

    for t in range(tiles):
        rows = slice(t * QB, (t + 1) * QB)
        win = slice(t * QB, t * QB + reach)
        q_stack = stacked(q_ref[rows].astype(jnp.float32) * (HD ** -0.5))
        g_tile = g_ref[rows].astype(jnp.float32)
        g_stack = stacked(g_tile)
        g_t = g_tile.T
        s = dot(kwin[win], q_stack, 1, 1)
        blocks = []
        for j in range(REACH):
            bias = jnp.where(allow_ref[(tiles if high else 0) + t, j] > 0, 0.0, NEG)
            block = s[j * QB : (j + 1) * QB] + bias
            if j == REACH - 1:
                block = block + causal
            blocks.append(block)
        s = jnp.concatenate(blocks, axis=0)
        row_max = jnp.max(s, axis=0, keepdims=True)
        p = jnp.exp(s - row_max)
        total = jnp.sum(p, axis=0, keepdims=True)
        inv = 1.0 / total
        p_round = p.astype(jnp.bfloat16)
        att_parts = []
        delta_parts = []
        for h in range(heads):
            cols = slice(h * QB, (h + 1) * QB)
            feats = slice(h * HD, (h + 1) * HD)
            mix = dot(vt[feats, win], p_round[:, cols], 1, 0) * inv[:, cols]
            mix = mix.astype(jnp.bfloat16).astype(jnp.float32)
            att_parts.append(mix)
            delta_parts.append(jnp.sum(mix * g_t[feats], axis=0, keepdims=True))
        att_ref[rows] = jnp.concatenate(att_parts, axis=0).T.astype(jnp.bfloat16)
        delta = jnp.concatenate(delta_parts, axis=1)
        back = p * inv
        dv[win] += dot(back.astype(jnp.bfloat16), g_stack, 1, 0)
        dprob = dot(vwin[win], g_stack, 1, 1)
        ds = (back * (dprob - delta)).astype(jnp.bfloat16)
        dk[win] += dot(ds, q_stack, 1, 0)
        dq_parts = []
        for h in range(heads):
            cols = slice(h * QB, (h + 1) * QB)
            feats = slice(h * HD, (h + 1) * HD)
            dq_parts.append(dot(kt[feats, win], ds[:, cols], 1, 0))
        dq_ref[rows] = (jnp.concatenate(dq_parts, axis=0).T * (HD ** -0.5)).astype(jnp.bfloat16)
    dkvp_ref[:span] = dk[:span].astype(jnp.bfloat16)
    dkvp_ref[span:] = dv[:span].astype(jnp.bfloat16)
    dko_ref[...] = dk[span:]
    dvo_ref[...] = dv[span:]


def attention(allow, flag, queries, keys, values, kv_before, grad_attn, high):
    rows, width = queries.shape
    span = rows // 2
    half = 1 if high else 0
    own = pl.BlockSpec((span, width), lambda i: (half, 0))
    low = pl.BlockSpec((span, width), lambda i: (0, 0))
    both = pl.BlockSpec((2 * span, width), lambda i: (0, 0))
    smem = pl.BlockSpec(memory_space=pltpu.SMEM)
    return pl.pallas_call(
        functools.partial(attention_kernel, high=high),
        grid=(1,),
        in_specs=[smem, smem, own, own, own, both, low, low, own],
        out_specs=[low, low, both, low, low],
        out_shape=[
            jax.ShapeDtypeStruct((span, width), jnp.bfloat16),
            jax.ShapeDtypeStruct((span, width), jnp.bfloat16),
            jax.ShapeDtypeStruct((2 * span, width), jnp.bfloat16),
            jax.ShapeDtypeStruct((span, width), jnp.float32),
            jax.ShapeDtypeStruct((span, width), jnp.float32),
        ],
        scratch_shapes=[
            pltpu.VMEM((2 * span, width), jnp.bfloat16),
            pltpu.VMEM((2 * span, width), jnp.bfloat16),
            pltpu.VMEM((width, 2 * span), jnp.bfloat16),
            pltpu.VMEM((width, 2 * span), jnp.bfloat16),
            pltpu.VMEM((2 * span, width), jnp.float32),
            pltpu.VMEM((2 * span, width), jnp.float32),
        ],
        compiler_params=pltpu.CompilerParams(vmem_limit_bytes=48 * 1024 * 1024),
        name="attention_high" if high else "attention_low",
    )(allow, flag, queries, keys, values, kv_before, keys, values, grad_attn)


def output_kernel(*refs):
    out_ref = refs[-1]
    count = (len(refs) - 1) // 3
    weights = refs[2 * count : 3 * count]
    span = refs[0].shape[0]
    for half in range(2):
        parts = refs[half * count : (half + 1) * count]
        total = dot(parts[0][...], weights[0][...], 1, 0)
        for part, weight in zip(parts[1:], weights[1:]):
            total = total + dot(part[...], weight[...], 1, 0)
        out_ref[half * span : (half + 1) * span] = total.astype(jnp.bfloat16)


def shifted(x, by):
    devices = lax.axis_size("tm")
    return lax.ppermute(
        x, "tm", [(i, i + by) for i in range(devices) if 0 <= i + by < devices]
    )


def swapped(x, bit):
    devices = lax.axis_size("head")
    return lax.ppermute(x, "head", [(i, i ^ bit) for i in range(devices)])


def on_device(queries, keys, values, out_weight, grad_output, tile_lists):
    rows, width = queries.shape
    span = rows // 2
    tiles = span // QB
    tm_count = lax.axis_size("tm")
    tm_index = lax.axis_index("tm")
    head_index = lax.axis_index("head")
    is_last = tm_index == tm_count - 1
    token_total = tm_count * rows
    model = out_weight.shape[1]

    kv_low = shifted(jnp.concatenate([keys[:span], values[:span]], axis=0), 1)
    kv_high = shifted(jnp.concatenate([keys[span:], values[span:]], axis=0), -1)

    def weight_cols(head):
        return lax.dynamic_slice_in_dim(out_weight, head * width, width, axis=1)

    weights = [weight_cols(head_index)] + [
        swapped(weight_cols(head_index ^ bit), bit) for bit in (1, 2, 3)
    ]

    pieces = jnp.stack([tm_index, 2 * tm_count - 1 - tm_index])
    tile_ids = (pieces[:, None] * tiles + jnp.arange(tiles, dtype=jnp.int32)).reshape(-1)
    wanted = tile_ids[:, None] - (REACH - 1) + jnp.arange(REACH, dtype=jnp.int32)
    allow = jnp.any(
        (tile_lists[:, :, None] == wanted[:, None, :]) & (tile_lists[:, :, None] >= 0), axis=1
    ).astype(jnp.int32)
    flag = is_last.astype(jnp.int32).reshape(1)

    grad_attn = lax.dot_general(
        grad_output, out_weight, (((1,), (1,)), ((), ())), preferred_element_type=jnp.float32
    ).astype(jnp.bfloat16)

    gathered = []
    results = []
    for kv_before, high in ((kv_low, False), (kv_high, True)):
        att, dq, dkvp, dko, dvo = attention(
            allow, flag, queries, keys, values, kv_before, grad_attn, high
        )
        across = swapped(att, 2)
        gathered.append([att, swapped(att, 1), across, swapped(across, 1)])
        results.append((att, dq, dkvp, dko, dvo))
    (att_l, dq_l, dkvp_l, dko_l, dvo_l), (att_h, dq_h, dkvp_h, dko_h, dvo_h) = results
    back_low = shifted(dkvp_l, -1)
    back_high = shifted(dkvp_h, 1)

    attended = jnp.concatenate([att_l, att_h], axis=0)
    weight_term = lax.dot_general(
        grad_output, attended, (((0,), (0,)), ((), ())), preferred_element_type=jnp.float32
    ).astype(jnp.bfloat16)
    exchanged = lax.all_to_all(
        weight_term.reshape(tm_count, model // tm_count, width), "tm", 0, 0
    )
    grad_weight = (
        jnp.sum(exchanged.astype(jnp.float32), axis=0) * token_total ** (-0.5)
    ).T

    output = pl.pallas_call(
        output_kernel,
        out_shape=jax.ShapeDtypeStruct((rows, width), jnp.bfloat16),
        name="output",
    )(*gathered[0], *gathered[1], *weights)

    low_add = jnp.where(is_last, dkvp_h, back_low).astype(jnp.float32)
    high_add = back_high.astype(jnp.float32)
    grad_keys = jnp.concatenate([dko_l + low_add[:span], dko_h + high_add[:span]], axis=0)
    grad_values = jnp.concatenate([dvo_l + low_add[span:], dvo_h + high_add[span:]], axis=0)
    grad_queries = jnp.concatenate([dq_l, dq_h], axis=0)
    return (
        output,
        grad_queries,
        grad_keys.astype(jnp.bfloat16),
        grad_values.astype(jnp.bfloat16),
        grad_weight,
    )


def solution(mesh):
    return jax.shard_map(
        on_device,
        mesh=mesh,
        in_specs=(
            P("tm", "head"),
            P("tm", "head"),
            P("tm", "head"),
            P("head", None),
            P("tm", None),
            P("tm", None),
        ),
        out_specs=(
            P("tm", "head"),
            P("tm", "head"),
            P("tm", "head"),
            P("tm", "head"),
            P("head", "tm"),
        ),
        check_vma=False,
    )
```

time: 282 us -> 103 us (0.37)
  waiting for transfers between devices: 154 us -> 23.2 us
  matrix products: 30.4 us -> 3.42 us
  Pallas kernels: 0 us -> 15.7 us
  between operations: 14.8 us -> 0.95 us
  other arithmetic: 20.8 us -> 8.77 us
  local copies, waits for them, and re-layouts: 25.2 us -> 14.4 us
    reduce_scatter x2 -> x0, waiting for transfers between devices: 146 us -> none  [the longest x1 82.3 us: on_device(): lax.psum_scatter(weight_term, 'tm', scatter_dimension=1, tiled=True)]
    dot_general x14 -> x1, matrix products: 28.9 us -> 1.52 us  [on_device(): lax.dot_general(grad_output, attended, (((0,), (0,)), ((), ())), preferre...]
    pallas_call x0 -> x3, Pallas kernels: none -> 15.7 us  [the longest x2 12.6 us: attention(): pl.pallas_call(functools.partial(attention_kernel, high=high), grid=(1,),...]
    ppermute x8 -> x13, waiting for transfers between devices: 8.2 us -> 23.2 us  [the longest x4 20.3 us: shifted(): lax.ppermute(x, 'tm', [(i, i + by) for i in range(devices) if 0 <= i + by...]
    all_to_all x0 -> x1, starting transfers between devices: none -> 10.8 us  [on_device(): lax.all_to_all(weight_term.reshape(tm_count, model // tm_count, width), '...]
    ppermute x8 -> x13, starting transfers between devices: 34.2 us -> 25.7 us  [the longest x4 15.6 us: shifted(): lax.ppermute(x, 'tm', [(i, i + by) for i in range(devices) if 0 <= i + by...]
    another operation x6 -> x2, other arithmetic: 8.31 us -> 0.33 us
    reshape x4 -> x0, local copies, waits for them, and re-layouts: 5.66 us -> none  [the longest x2 3.36 us: on_device(): g_half = grad_attn.reshape(2, span_rows, local_heads, HD)]
  transfers between devices with their start and end apart: 10 -> 14, of which waited for: 4 -> 4; matrix products, arithmetic and copies ran while one was open for 23% -> 12% of each run, Pallas kernels for 0% -> 6%
where the time goes in v1:
time: 103 us
  starting transfers between devices  36.4 us (35%)
  waiting for transfers between devices  23.2 us (23%)
  Pallas kernels  15.7 us (15%)
  local copies, waits for them, and re-layouts  14.4 us (14%)
  other arithmetic  8.77 us (9%)
  matrix products  3.42 us (3%)
    ppermute x4, waiting for transfers between devices, shifted(): lax.ppermute(x, 'tm', [(i, i + by) for i in range(devices) if 0 <= i + by...  20.3 us
    ppermute x4, starting transfers between devices, shifted(): lax.ppermute(x, 'tm', [(i, i + by) for i in range(devices) if 0 <= i + by...  15.6 us
    pallas_call x2, Pallas kernels, attention(): pl.pallas_call(functools.partial(attention_kernel, high=high), grid=(1,),...  12.6 us
    all_to_all x1, starting transfers between devices, on_device(): lax.all_to_all(weight_term.reshape(tm_count, model // tm_count, width), '...  10.8 us
    ppermute x9, starting transfers between devices, swapped(): return lax.ppermute(x, 'head', [(i, i ^ bit) for i in range(devices)])  10 us
    unnamed x51, local copies, waits for them, and re-layouts  8.79 us
    pallas_call x1, Pallas kernels, on_device(): pl.pallas_call(output_kernel, out_shape=jax.ShapeDtypeStruct((rows, width...  3.16 us
    ppermute x9, waiting for transfers between devices, swapped(): return lax.ppermute(x, 'head', [(i, i ^ bit) for i in range(devices)])  2.87 us
  transfers between devices with their start and end apart: 14, of which 4 were waited for; matrix products, arithmetic and copies ran while one was open for 12% of the time, Pallas kernels for 6%

profile of v1, /device:TPU:32, one launch (start us, length us, event | category | flops | bytes accessed | tf_op | source)
XLA Modules:
  0.0 102.8 jit_solution(15700151026928956158)
XLA Ops:
  0.7 1.4 %fusion.9 = (bf16[512,256]{1,0:T(8,128)(2,1)S(1)}, bf16[512,256]{1,0:T(8,128)(2,1)S(1)}, bf16[512,256]{1,0:T(8,128)(2,1)S(1)}, bf16[512,256]{1,0:T(8,128)(2,1)S(1)}) fusion(bf16[1024,256]{1,0:T(8,128)(2,1)} %kl_ref.3, bf16[1024,256]{1,0:T(8,128)(2,1)} %vl_ref.3), kind=kLoop, calls=%fused_computation.32 | loop fusion | bytes 2097152 | tf_op jit(solution)/shard_map/slice | solution.py:178
  2.1 0.8 pad_maximum_fusion.1
  2.9 5.4 %collective-permute-start.4 = (bf16[1024,256]{1,0:T(8,128)(2,1)}, bf16[1024,256]{1,0:T(8,128)(2,1)S(1)}, u32[]{:S(2)}, u32[]{:S(2)}) collective-permute-start(bf16[1024,256]{1,0:T(8,128)(2,1)} %pad_maximum_fusion.1), channel_id=1, source_target_pairs={{4,0},{8,4},{12,8},{16,12},{20,16},{24,20},{28,24},{32,28},{36,32}... | collective-permute-start | bytes 1572872 | tf_op jit(solution)/shard_map/ppermute | solution.py:156
  8.3 0.8 pad_maximum_fusion
  9.1 1.9 %collective-permute-start = (bf16[1024,256]{1,0:T(8,128)(2,1)}, bf16[1024,256]{1,0:T(8,128)(2,1)}, u32[]{:S(2)}, u32[]{:S(2)}) collective-permute-start(bf16[1024,256]{1,0:T(8,128)(2,1)} %pad_maximum_fusion), channel_id=1, source_target_pairs={{0,4},{4,8},{8,12},{12,16},{16,20},{20,24},{24,28},{28,32},{32,36}... | collective-permute-start | bytes 1572872 | tf_op jit(solution)/shard_map/ppermute | solution.py:156
  11.7 1.9 %convolution_convert_fusion.1.g_ref = bf16[1024,256]{1,0:T(8,128)(2,1)S(1)} fusion(bf16[1024,1024]{1,0:T(8,128)(2,1)S(1)} %copy-done, bf16[256,1024]{1,0:T(8,128)(2,1)} %param.9), kind=kOutput, calls=%fused_computation.1 | convolution fusion | flops 537133056 | bytes 3145728 | tf_op jit(solution)/shard_map/dot_general | solution.py:195
  13.6 6.2 %collective-permute-done.4.kvp_ref = bf16[1024,256]{1,0:T(8,128)(2,1)S(1)} collective-permute-done((bf16[1024,256]{1,0:T(8,128)(2,1)}, bf16[1024,256]{1,0:T(8,128)(2,1)S(1)}, u32[]{:S(2)}, u32[]{:S(2)}) %collective-permute-start.4) | collective-permute-done | bytes 524320 | tf_op jit(solution)/shard_map/ppermute | solution.py:156
  19.8 0.8 copy-done.13
  20.6 1.0 %copy-done.14 = bf16[1024,256]{1,0:T(8,128)(2,1)S(1)} copy-done((bf16[1024,256]{1,0:T(8,128)(2,1)S(1)}, bf16[1024,256]{1,0:T(8,128)(2,1)}, u32[]{:S(2)}) %copy-start.14) | copy-done | bytes 524312
  21.6 6.0 %attention_high.1 = (bf16[512,256]{1,0:T(8,128)(2,1)S(1)}, bf16[512,256]{1,0:T(8,128)(2,1)S(1)}, bf16[1024,256]{1,0:T(8,128)(2,1)S(1)}, f32[512,256]{1,0:T(8,128)S(1)}, f32[512,256]{1,0:T(8,128)S(1)}) custom-call(s32[8,5]{1,0:T(8,128)S(1)} %convert_element_type.24.allow_ref, s32[1]{0:T(128)} %bitcast.2.flag_ref, bf16[1024,256]{1,0:T(8,128)(2,1)S(1)} %copy-done.3, ...), custom_call_target="tpu_custom_call" | custom-call | tf_op jit(solution)/shard_map/attention_high/pallas_call | solution.py:116
  28.4 0.8 copy-done.8
  29.2 6.5 %attention_low.1 = (bf16[512,256]{1,0:T(8,128)(2,1)S(1)}, bf16[512,256]{1,0:T(8,128)(2,1)S(1)}, bf16[1024,256]{1,0:T(8,128)(2,1)S(1)}, f32[512,256]{1,0:T(8,128)S(1)}, f32[512,256]{1,0:T(8,128)S(1)}) custom-call(s32[8,5]{1,0:T(8,128)S(1)} %convert_element_type.24.allow_ref, s32[1]{0:T(128)} %bitcast.2.flag_ref, bf16[1024,256]{1,0:T(8,128)(2,1)S(1)} %copy-done.3, ...), custom_call_target="tpu_custom_call" | custom-call | tf_op jit(solution)/shard_map/attention_low/pallas_call | solution.py:116
  38.1 0.8 copy-done.16
  38.9 1.5 %fusion = bf16[1024,256]{0,1:T(8,128)(2,1)} fusion(bf16[1024,1024]{1,0:T(8,128)(2,1)S(1)} %copy-done, bf16[512,256]{1,0:T(8,128)(2,1)S(1)} %get-tuple-element.16.refs_4_, bf16[512,256]{1,0:T(8,128)(2,1)S(1)} %get-tuple-element.15.refs_0_), kind=kOutput, calls=%fused_computation.2 | convolution fusion | flops 538181632 | bytes 3145728 | tf_op jit(solution)/shard_map/dot_general | solution.py:213
  40.4 2.0 %copy.14 = bf16[1024,256]{1,0:T(8,128)(2,1)} copy(bf16[1024,256]{0,1:T(8,128)(2,1)} %fusion) | data formatting | bytes 1048576 | tf_op jit(solution)/shard_map/convert_element_type | solution.py:215
  42.5 10.8 %all-to-all-start = ((bf16[32,32,256]{2,1,0:T(8,128)(2,1)}), bf16[32,32,256]{2,1,0:T(8,128)(2,1)}, u32[]{:S(2)}, u32[]{:S(2)}) async-start(bf16[32,32,256]{2,1,0:T(8,128)(2,1)} %bitcast.11), calls=%async_computation | async-start | bytes 1048576 | tf_op jit(solution)/shard_map/all_to_all | solution.py:216
  53.2 5.5 %collective-permute-start.11 = (bf16[1024,256]{1,0:T(8,128)(2,1)}, bf16[1024,256]{1,0:T(8,128)(2,1)}, u32[]{:S(2)}, u32[]{:S(2)}) collective-permute-start(bf16[1024,256]{1,0:T(8,128)(2,1)} %copy-done.16), channel_id=1, source_target_pairs={{4,0},{8,4},{12,8},{16,12},{20,16},{24,20},{28,24},{32,28},{36,32}... | collective-permute-start | bytes 1572872 | tf_op jit(solution)/shard_map/ppermute | solution.py:156
  58.7 1.9 %constant_dynamic-slice_fusion = (bf16[256,256]{1,0:T(8,128)(2,1)}, bf16[256,256]{1,0:T(8,128)(2,1)}, bf16[256,256]{1,0:T(8,128)(2,1)}, bf16[256,256]{1,0:T(8,128)(2,1)}) fusion(bf16[256,1024]{1,0:T(8,128)(2,1)} %param.9, s32[]{:T(128)S(6)} %select_n.23, s32[]{:T(128)S(6)} %select_n.21, s32[]{:T(128)S(6)} %select_n.20, s32[]{:T(128)S(6)} %select_n.22), kind=kLoop, calls=%fused_computation.25 | loop fusion | bytes 1048592 | tf_op jit(solution)/shard_map/dynamic_slice | solution.py:181
  61.1 2.4 %collective-permute-start.8 = (bf16[256,256]{1,0:T(8,128)(2,1)}, bf16[256,256]{1,0:T(8,128)(2,1)}, u32[]{:S(2)}, u32[]{:S(2)}) collective-permute-start(bf16[256,256]{1,0:T(8,128)(2,1)} %get-tuple-element.30), channel_id=1, source_target_pairs={{0,1},{1,0},{2,3},{3,2},{4,5},{5,4},{6,7},{7,6},{8,9},{9,8},{10,11... | collective-permute-start | bytes 393224 | tf_op jit(solution)/shard_map/ppermute | solution.py:163
  63.5 0.8 collective-permute-start.6
  64.3 2.7 %collective-permute-start.2 = (bf16[512,256]{1,0:T(8,128)(2,1)S(1)}, bf16[512,256]{1,0:T(8,128)(2,1)}, u32[]{:S(2)}, u32[]{:S(2)}) collective-permute-start(bf16[512,256]{1,0:T(8,128)(2,1)S(1)} %get-tuple-element.15.refs_0_), channel_id=1, source_target_pairs={{0,2},{1,3},{2,0},{3,1},{4,6},{5,7},{6,4},{7,5},{8,10},{9,11},{10,... | collective-permute-start | bytes 786440 | tf_op jit(solution)/shard_map/ppermute | solution.py:163
  67.0 1.8 %pad_maximum_fusion.2 = bf16[1024,256]{1,0:T(8,128)(2,1)} fusion(bf16[512,256]{1,0:T(8,128)(2,1)S(1)} %get-tuple-element.18, bf16[512,256]{1,0:T(8,128)(2,1)} %copy-done.15), kind=kLoop, calls=%fused_computation.14 | loop fusion | flops 1048576 | bytes 1048576 | tf_op jit(solution)/shard_map/concatenate | solution.py:233
  68.8 1.2 %convert_reduce_fusion = f32[32,256]{1,0:T(8,128)S(1)} fusion(bf16[32,32,256]{2,1,0:T(8,128)(2,1)} %all-to-all-done), kind=kLoop, calls=%fused_computation.3 | loop fusion | flops 516096 | bytes 557056 | tf_op jit(solution)/shard_map/reduce_sum | solution.py:220
  70.6 1.1 %collective-permute-done.11 = bf16[1024,256]{1,0:T(8,128)(2,1)} collective-permute-done((bf16[1024,256]{1,0:T(8,128)(2,1)}, bf16[1024,256]{1,0:T(8,128)(2,1)}, u32[]{:S(2)}, u32[]{:S(2)}) %collective-permute-start.11) | collective-permute-done | bytes 524320 | tf_op jit(solution)/shard_map/ppermute | solution.py:156
  71.8 2.9 %collective-permute-start.12 = (bf16[1024,256]{1,0:T(8,128)(2,1)}, bf16[1024,256]{1,0:T(8,128)(2,1)S(1)}, u32[]{:S(2)}, u32[]{:S(2)}) collective-permute-start(bf16[1024,256]{1,0:T(8,128)(2,1)} %copy-done.8), channel_id=1, source_target_pairs={{0,4},{4,8},{8,12},{12,16},{16,20},{20,24},{24,28},{28,32},{32,36}... | collective-permute-start | bytes 1572872 | tf_op jit(solution)/shard_map/ppermute | solution.py:156
  74.7 1.1 %select_convert_fusion = f32[1024,256]{1,0:T(8,128)S(1)} fusion(bf16[1024,256]{1,0:T(8,128)(2,1)} %copy-done.8, bf16[1024,256]{1,0:T(8,128)(2,1)} %collective-permute-done.11, pred[]{:T(512)S(6)} %eq.19), kind=kLoop, calls=%fused_computation.20 | loop fusion | flops 524288 | bytes 2097153 | tf_op jit(solution)/shard_map/convert_element_type | solution.py:229
  76.0 13.0 %collective-permute-done.12 = bf16[1024,256]{1,0:T(8,128)(2,1)S(1)} collective-permute-done((bf16[1024,256]{1,0:T(8,128)(2,1)}, bf16[1024,256]{1,0:T(8,128)(2,1)S(1)}, u32[]{:S(2)}, u32[]{:S(2)}) %collective-permute-start.12) | collective-permute-done | bytes 524320 | tf_op jit(solution)/shard_map/ppermute | solution.py:156
  90.4 2.6 %collective-permute-start.9 = (bf16[256,256]{1,0:T(8,128)(2,1)S(1)}, bf16[256,256]{1,0:T(8,128)(2,1)S(1)}, u32[]{:S(2)}, u32[]{:S(2)}) collective-permute-start(bf16[256,256]{1,0:T(8,128)(2,1)S(1)} %copy-done.23), channel_id=1, source_target_pairs={{0,2},{1,3},{2,0},{3,1},{4,6},{5,7},{6,4},{7,5},{8,10},{9,11},{10,... | collective-permute-start | bytes 393224 | tf_op jit(solution)/shard_map/ppermute | solution.py:163
  93.0 0.8 pad_maximum_fusion.4
  93.8 0.8 pad_maximum_fusion.3
  94.7 2.8 %collective-permute-done.9.refs_10_ = bf16[256,256]{1,0:T(8,128)(2,1)S(1)} collective-permute-done((bf16[256,256]{1,0:T(8,128)(2,1)S(1)}, bf16[256,256]{1,0:T(8,128)(2,1)S(1)}, u32[]{:S(2)}, u32[]{:S(2)}) %collective-permute-start.9) | collective-permute-done | bytes 131104 | tf_op jit(solution)/shard_map/ppermute | solution.py:163
  99.7 3.2 %output.1 = bf16[1024,256]{1,0:T(8,128)(2,1)} custom-call(bf16[512,256]{1,0:T(8,128)(2,1)} %copy-done.5, bf16[512,256]{1,0:T(8,128)(2,1)} %copy-done.18, bf16[512,256]{1,0:T(8,128)(2,1)} %collective-permute-done.2.refs_2_, bf16[512,256]{1,0:T(8,128)(2,1)} %copy-done.20, bf16[512,256]{1,0:T(8,128)(2,1)} %copy-done.4, bf16[512,256]{1,0:T(8,128)(2,1)} %copy-done.17, ...), custom_call_target="tpu_custom_call" | custom-call | tf_op jit(solution)/shard_map/output/pallas_call | solution.py:223
  (74 shorter events, 8.5 us)
Async XLA Ops:
  0.6 11.0 %copy-start = (bf16[1024,1024]{1,0:T(8,128)(2,1)S(1)}, bf16[1024,1024]{1,0:T(8,128)(2,1)}, u32[]{:S(2)}) copy-start(bf16[1024,1024]{1,0:T(8,128)(2,1)} %param.10) | copy-start | bytes 6291460
  0.6 10.6 %copy-start.24 = (s32[8,5]{1,0:T(8,128)S(1)}, s32[8,5]{1,0:T(8,128)}, u32[]{:S(2)}) copy-start(s32[8,5]{1,0:T(8,128)} %param.11) | copy-start | bytes 484
  2.9 16.9 %collective-permute-start.4 = (bf16[1024,256]{1,0:T(8,128)(2,1)}, bf16[1024,256]{1,0:T(8,128)(2,1)S(1)}, u32[]{:S(2)}, u32[]{:S(2)}) collective-permute-start(bf16[1024,256]{1,0:T(8,128)(2,1)} %pad_maximum_fusion.1), channel_id=1, source_target_pairs={{4,0},{8,4},{12,8},{16,12},{20,16},{24,20},{28,24},{32,28},{36,32}... | collective-permute-start | bytes 1572872 | tf_op jit(solution)/shard_map/ppermute | solution.py:156
  9.1 20.1 %collective-permute-start = (bf16[1024,256]{1,0:T(8,128)(2,1)}, bf16[1024,256]{1,0:T(8,128)(2,1)}, u32[]{:S(2)}, u32[]{:S(2)}) collective-permute-start(bf16[1024,256]{1,0:T(8,128)(2,1)} %pad_maximum_fusion), channel_id=1, source_target_pairs={{0,4},{4,8},{8,12},{12,16},{16,20},{20,24},{24,28},{28,32},{32,36}... | collective-permute-start | bytes 1572872 | tf_op jit(solution)/shard_map/ppermute | solution.py:156
  11.6 8.9 %copy-start.1 = (bf16[1024,256]{1,0:T(8,128)(2,1)S(1)}, bf16[1024,256]{1,0:T(8,128)(2,1)}, u32[]{:S(2)}) copy-start(bf16[1024,256]{1,0:T(8,128)(2,1)} %kl_ref.3) | copy-start | bytes 1572868
  11.7 8.9 %copy-start.2 = (bf16[1024,256]{1,0:T(8,128)(2,1)S(1)}, bf16[1024,256]{1,0:T(8,128)(2,1)}, u32[]{:S(2)}) copy-start(bf16[1024,256]{1,0:T(8,128)(2,1)} %vl_ref.3) | copy-start | bytes 1572868
  11.7 8.9 %copy-start.3 = (bf16[1024,256]{1,0:T(8,128)(2,1)S(1)}, bf16[1024,256]{1,0:T(8,128)(2,1)}, u32[]{:S(2)}) copy-start(bf16[1024,256]{1,0:T(8,128)(2,1)} %q_ref.3) | copy-start | bytes 1572868
  20.6 1.0 %copy-start.14 = (bf16[1024,256]{1,0:T(8,128)(2,1)S(1)}, bf16[1024,256]{1,0:T(8,128)(2,1)}, u32[]{:S(2)}) copy-start(bf16[1024,256]{1,0:T(8,128)(2,1)} %copy-done.13) | copy-start | bytes 1572868
  27.6 0.8 copy-start.6
  29.2 59.8 %copy-start.4 = (bf16[512,256]{1,0:T(8,128)(2,1)}, bf16[512,256]{1,0:T(8,128)(2,1)S(1)}, u32[]{:S(2)}) copy-start(bf16[512,256]{1,0:T(8,128)(2,1)S(1)} %get-tuple-element.16.refs_4_) | copy-start | bytes 786436
  35.8 0.8 copy-start.9
  38.1 0.8 copy-start.16
  38.9 50.2 %copy-start.5 = (bf16[512,256]{1,0:T(8,128)(2,1)}, bf16[512,256]{1,0:T(8,128)(2,1)S(1)}, u32[]{:S(2)}) copy-start(bf16[512,256]{1,0:T(8,128)(2,1)S(1)} %get-tuple-element.15.refs_0_) | copy-start | bytes 786436
  42.5 26.3 %all-to-all-start = ((bf16[32,32,256]{2,1,0:T(8,128)(2,1)}), bf16[32,32,256]{2,1,0:T(8,128)(2,1)}, u32[]{:S(2)}, u32[]{:S(2)}) async-start(bf16[32,32,256]{2,1,0:T(8,128)(2,1)} %bitcast.11), calls=%async_computation | async-start | bytes 1048576 | tf_op jit(solution)/shard_map/all_to_all | solution.py:216
  53.2 18.6 %collective-permute-start.11 = (bf16[1024,256]{1,0:T(8,128)(2,1)}, bf16[1024,256]{1,0:T(8,128)(2,1)}, u32[]{:S(2)}, u32[]{:S(2)}) collective-permute-start(bf16[1024,256]{1,0:T(8,128)(2,1)} %copy-done.16), channel_id=1, source_target_pairs={{4,0},{8,4},{12,8},{16,12},{20,16},{24,20},{28,24},{32,28},{36,32}... | collective-permute-start | bytes 1572872 | tf_op jit(solution)/shard_map/ppermute | solution.py:156
  60.6 28.5 %collective-permute-start.10 = (bf16[256,256]{1,0:T(8,128)(2,1)}, bf16[256,256]{1,0:T(8,128)(2,1)S(1)}, u32[]{:S(2)}, u32[]{:S(2)}) collective-permute-start(bf16[256,256]{1,0:T(8,128)(2,1)} %get-tuple-element.29), channel_id=1, source_target_pairs={{0,3},{1,2},{2,1},{3,0},{4,7},{5,6},{6,5},{7,4},{8,11},{9,10},{10,... | collective-permute-start | bytes 393224 | tf_op jit(solution)/shard_map/ppermute | solution.py:163
  61.1 29.3 %collective-permute-start.8 = (bf16[256,256]{1,0:T(8,128)(2,1)}, bf16[256,256]{1,0:T(8,128)(2,1)}, u32[]{:S(2)}, u32[]{:S(2)}) collective-permute-start(bf16[256,256]{1,0:T(8,128)(2,1)} %get-tuple-element.30), channel_id=1, source_target_pairs={{0,1},{1,0},{2,3},{3,2},{4,5},{5,4},{6,7},{7,6},{8,9},{9,8},{10,11... | collective-permute-start | bytes 393224 | tf_op jit(solution)/shard_map/ppermute | solution.py:163
  63.5 26.2 %collective-permute-start.6 = (bf16[512,256]{1,0:T(8,128)(2,1)S(1)}, bf16[512,256]{1,0:T(8,128)(2,1)}, u32[]{:S(2)}, u32[]{:S(2)}) collective-permute-start(bf16[512,256]{1,0:T(8,128)(2,1)S(1)} %get-tuple-element.16.refs_4_), channel_id=1, source_target_pairs={{0,2},{1,3},{2,0},{3,1},{4,6},{5,7},{6,4},{7,5},{8,10},{9,11},{10,... | collective-permute-start | bytes 786440 | tf_op jit(solution)/shard_map/ppermute | solution.py:163
  64.3 25.5 %collective-permute-start.2 = (bf16[512,256]{1,0:T(8,128)(2,1)S(1)}, bf16[512,256]{1,0:T(8,128)(2,1)}, u32[]{:S(2)}, u32[]{:S(2)}) collective-permute-start(bf16[512,256]{1,0:T(8,128)(2,1)S(1)} %get-tuple-element.15.refs_0_), channel_id=1, source_target_pairs={{0,2},{1,3},{2,0},{3,1},{4,6},{5,7},{6,4},{7,5},{8,10},{9,11},{10,... | collective-permute-start | bytes 786440 | tf_op jit(solution)/shard_map/ppermute | solution.py:163
  68.8 7.0 %copy-start.10 = (f32[512,256]{1,0:T(8,128)S(1)}, f32[512,256]{1,0:T(8,128)}, u32[]{:S(2)}) copy-start(f32[512,256]{1,0:T(8,128)} %copy-done.9) | copy-start | bytes 1572868
  68.8 7.0 %copy-start.12 = (f32[512,256]{1,0:T(8,128)S(1)}, f32[512,256]{1,0:T(8,128)}, u32[]{:S(2)}) copy-start(f32[512,256]{1,0:T(8,128)} %copy-done.11) | copy-start | bytes 1572868
  71.8 17.2 %collective-permute-start.12 = (bf16[1024,256]{1,0:T(8,128)(2,1)}, bf16[1024,256]{1,0:T(8,128)(2,1)S(1)}, u32[]{:S(2)}, u32[]{:S(2)}) collective-permute-start(bf16[1024,256]{1,0:T(8,128)(2,1)} %copy-done.8), channel_id=1, source_target_pairs={{0,4},{4,8},{8,12},{12,16},{16,20},{20,24},{24,28},{28,32},{32,36}... | collective-permute-start | bytes 1572872 | tf_op jit(solution)/shard_map/ppermute | solution.py:156
  75.8 14.4 %copy-start.7 = (f32[512,256]{1,0:T(8,128)S(1)}, f32[512,256]{1,0:T(8,128)}, u32[]{:S(2)}) copy-start(f32[512,256]{1,0:T(8,128)} %copy-done.6) | copy-start | bytes 1572868
  76.0 14.4 %copy-start.23 = (bf16[256,256]{1,0:T(8,128)(2,1)S(1)}, bf16[256,256]{1,0:T(8,128)(2,1)}, u32[]{:S(2)}) copy-start(bf16[256,256]{1,0:T(8,128)(2,1)} %get-tuple-element.32) | copy-start | bytes 393220
  89.0 8.5 %collective-permute-start.5 = (bf16[512,256]{1,0:T(8,128)(2,1)S(1)}, bf16[512,256]{1,0:T(8,128)(2,1)S(1)}, u32[]{:S(2)}, u32[]{:S(2)}) collective-permute-start(bf16[512,256]{1,0:T(8,128)(2,1)S(1)} %get-tuple-element.16.refs_4_), channel_id=1, source_target_pairs={{0,1},{1,0},{2,3},{3,2},{4,5},{5,4},{6,7},{7,6},{8,9},{9,8},{10,11... | collective-permute-start | bytes 786440 | tf_op jit(solution)/shard_map/ppermute | solution.py:163
  89.1 5.5 %copy-start.21 = (bf16[256,256]{1,0:T(8,128)(2,1)}, bf16[256,256]{1,0:T(8,128)(2,1)S(1)}, u32[]{:S(2)}) copy-start(bf16[256,256]{1,0:T(8,128)(2,1)S(1)} %collective-permute-done.10.refs_11_) | copy-start | bytes 393220
  89.1 8.4 %collective-permute-start.1 = (bf16[512,256]{1,0:T(8,128)(2,1)S(1)}, bf16[512,256]{1,0:T(8,128)(2,1)S(1)}, u32[]{:S(2)}, u32[]{:S(2)}) collective-permute-start(bf16[512,256]{1,0:T(8,128)(2,1)S(1)} %get-tuple-element.15.refs_0_), channel_id=1, source_target_pairs={{0,1},{1,0},{2,3},{3,2},{4,5},{5,4},{6,7},{7,6},{8,9},{9,8},{10,11... | collective-permute-start | bytes 786440 | tf_op jit(solution)/shard_map/ppermute | solution.py:163
  89.7 8.6 %collective-permute-start.7 = (bf16[512,256]{1,0:T(8,128)(2,1)}, bf16[512,256]{1,0:T(8,128)(2,1)S(1)}, u32[]{:S(2)}, u32[]{:S(2)}) collective-permute-start(bf16[512,256]{1,0:T(8,128)(2,1)} %collective-permute-done.6.refs_6_), channel_id=1, source_target_pairs={{0,1},{1,0},{2,3},{3,2},{4,5},{5,4},{6,7},{7,6},{8,9},{9,8},{10,11... | collective-permute-start | bytes 786440 | tf_op jit(solution)/shard_map/ppermute | solution.py:163
  89.8 9.2 %collective-permute-start.3 = (bf16[512,256]{1,0:T(8,128)(2,1)}, bf16[512,256]{1,0:T(8,128)(2,1)S(1)}, u32[]{:S(2)}, u32[]{:S(2)}) collective-permute-start(bf16[512,256]{1,0:T(8,128)(2,1)} %collective-permute-done.2.refs_2_), channel_id=1, source_target_pairs={{0,1},{1,0},{2,3},{3,2},{4,5},{5,4},{6,7},{7,6},{8,9},{9,8},{10,11... | collective-permute-start | bytes 786440 | tf_op jit(solution)/shard_map/ppermute | solution.py:163
  90.4 7.1 %collective-permute-start.9 = (bf16[256,256]{1,0:T(8,128)(2,1)S(1)}, bf16[256,256]{1,0:T(8,128)(2,1)S(1)}, u32[]{:S(2)}, u32[]{:S(2)}) collective-permute-start(bf16[256,256]{1,0:T(8,128)(2,1)S(1)} %copy-done.23), channel_id=1, source_target_pairs={{0,2},{1,3},{2,0},{3,1},{4,6},{5,7},{6,4},{7,5},{8,10},{9,11},{10,... | collective-permute-start | bytes 393224 | tf_op jit(solution)/shard_map/ppermute | solution.py:163
  97.5 2.2 %copy-start.22 = (bf16[256,256]{1,0:T(8,128)(2,1)}, bf16[256,256]{1,0:T(8,128)(2,1)S(1)}, u32[]{:S(2)}) copy-start(bf16[256,256]{1,0:T(8,128)(2,1)S(1)} %collective-permute-done.9.refs_10_) | copy-start | bytes 393220
  97.5 2.2 %copy-start.17 = (bf16[512,256]{1,0:T(8,128)(2,1)}, bf16[512,256]{1,0:T(8,128)(2,1)S(1)}, u32[]{:S(2)}) copy-start(bf16[512,256]{1,0:T(8,128)(2,1)S(1)} %collective-permute-done.5.refs_5_) | copy-start | bytes 786436
  (7 other events, 5.2 us)
